TPU v7x, 32 devices: a whole 2x2x4 slice. The times are simulated.
32 devices in a mesh: dp: 4 (over x, core), expert: 8 (over z, y).
Axes of the slice: x: 2, y: 2, z: 4, core: 2. Of those that a mesh axis runs over, the one named last changes fastest.
Arguments:
- tokens: bfloat16 [4096, 4096], P(('dp', 'expert')), may hold values from -6 to 6
- expert_ids: int32 [4096, 2], P(('dp', 'expert')), may hold values from 0 to 7, as said below
- gate_codes: int32 [4096, 2], P(('dp', 'expert')), may hold values from 1 to 64
- w_gate: bfloat16 [8, 4096, 768], P('expert'), may hold values from -0.09375 to 0.09375
- w_up: bfloat16 [8, 4096, 768], P('expert'), may hold values from -0.09375 to 0.09375
- w_down: bfloat16 [8, 768, 4096], P('expert'), may hold values from -0.21875 to 0.21875
- out_grad: bfloat16 [4096, 4096], P(('dp', 'expert')), may hold values from -6 to 6
Outputs:
- layer_out: bfloat16 [4096, 4096], P(('dp', 'expert'))
- tokens_grad: bfloat16 [4096, 4096], P(('dp', 'expert'))
- gate_weight_grad: bfloat16 [8, 4096, 768], P('expert', 'dp')
- up_weight_grad: bfloat16 [8, 4096, 768], P('expert', 'dp')
- down_weight_grad: bfloat16 [8, 768, 4096], P('expert', None, 'dp')
Inputs may be any that keep to these rules, and one draw needn't show every extreme that they name: `expert_ids`: each token names 2 different experts. In the rows of one device no expert is named more than 48 times, and in every draw one and the same expert is named exactly 48 times by the rows of every device.
All inputs are finite; a program needn't handle non-finite values.
Results may differ from a plain program's by a relative error of at most 0.009.
Values may be sent and summed in bfloat16 or wider, within the bound.
A program may use at most 192 MiB of HBM per device.

v0:
```python
import jax
import jax.numpy as jnp
from jax import lax
from jax.sharding import PartitionSpec as P


def slot_targets(block_ids, experts, capacity):
    flat_ids = block_ids.reshape(-1)
    one_hot = (flat_ids[:, None] == jnp.arange(experts, dtype=jnp.int32)[None, :]).astype(jnp.int32)
    earlier = jnp.cumsum(one_hot, axis=0) - one_hot
    slot_ranks = jnp.sum(earlier * one_hot, axis=1)
    return flat_ids * capacity + slot_ranks


def per_device(tokens, expert_ids, gate_codes, w_gate, w_up, w_down, out_grad):
    experts = lax.axis_size("expert")
    tok_count, model_width = tokens.shape
    top_count = expert_ids.shape[1]
    pair_count = tok_count * top_count
    capacity = 3 * pair_count // (2 * experts)
    targets = slot_targets(expert_ids, experts, capacity)
    owners = (
        jnp.full((experts * capacity,), -1, jnp.int32)
        .at[targets]
        .set(jnp.arange(pair_count, dtype=jnp.int32))
    )
    is_live = owners >= 0
    safe_pair = jnp.maximum(owners, 0)
    token_pos = safe_pair // top_count
    gate_flat = gate_codes.astype(jnp.float32).reshape(-1) / 64.0
    pair_gains = jnp.where(is_live, gate_flat[safe_pair], 0.0)
    outbound = jnp.where(is_live[:, None], tokens[token_pos], jnp.zeros((), jnp.bfloat16))
    outbound = outbound.reshape(experts, capacity, model_width)
    gate_matrix = w_gate[0]
    up_matrix = w_up[0]
    down_matrix = w_down[0]
    hidden_units = gate_matrix.shape[1]
    contract = (((1,), (1,)), ((), ()))
    contract_rows = (((0,), (0,)), ((), ()))
    received = lax.all_to_all(outbound, "expert", split_axis=0, concat_axis=0, tiled=True)
    slot_count = received.shape[1]
    expert_row_block = received.reshape(-1, model_width)
    pre_gate = jnp.dot(expert_row_block, gate_matrix, preferred_element_type=jnp.float32)
    pre_up = jnp.dot(expert_row_block, up_matrix, preferred_element_type=jnp.float32)
    expert_hidden = (pre_gate * jax.nn.sigmoid(pre_gate) * pre_up).astype(jnp.bfloat16)
    produced = jnp.dot(expert_hidden, down_matrix, preferred_element_type=jnp.float32).astype(
        jnp.bfloat16
    )
    produced = produced.reshape(experts, slot_count, model_width)
    returned = lax.all_to_all(produced, "expert", split_axis=0, concat_axis=0, tiled=True)
    returned, arrived, pre_gate, pre_up, hidden = (
        returned,
        received,
        pre_gate.reshape(experts, slot_count, hidden_units),
        pre_up.reshape(experts, slot_count, hidden_units),
        expert_hidden.reshape(experts, slot_count, hidden_units),
    )
    pair_out = returned.reshape(-1, model_width)[targets].astype(jnp.float32)
    weighted = gate_flat[:, None] * pair_out
    layer_out = jnp.sum(weighted.reshape(tok_count, top_count, model_width), axis=1).astype(
        jnp.bfloat16
    )
    upstream = out_grad[token_pos]
    pair_grad = (pair_gains[:, None] * upstream.astype(jnp.float32)).astype(jnp.bfloat16)
    pair_grad = pair_grad.reshape(experts, capacity, model_width)
    incoming = lax.all_to_all(pair_grad, "expert", split_axis=0, concat_axis=0, tiled=True).reshape(
        -1, model_width
    )
    pre_gate = pre_gate.reshape(-1, hidden_units)
    pre_up = pre_up.reshape(-1, hidden_units)
    hidden = hidden.reshape(-1, hidden_units)
    sigmoid_gate = jax.nn.sigmoid(pre_gate)
    silu_gate = pre_gate * sigmoid_gate
    hidden_grad = lax.dot_general(
        incoming, down_matrix, contract, preferred_element_type=jnp.float32
    )
    gate_pre_grad = (
        hidden_grad * pre_up * sigmoid_gate * (1.0 + pre_gate * (1.0 - sigmoid_gate))
    ).astype(jnp.bfloat16)
    up_pre_grad = (hidden_grad * silu_gate).astype(jnp.bfloat16)
    input_grad = lax.dot_general(
        gate_pre_grad, gate_matrix, contract, preferred_element_type=jnp.float32
    )
    input_grad = input_grad + lax.dot_general(
        up_pre_grad, up_matrix, contract, preferred_element_type=jnp.float32
    )
    input_grad = input_grad.astype(jnp.bfloat16).reshape(experts, capacity, model_width)
    returned_grad = lax.all_to_all(input_grad, "expert", split_axis=0, concat_axis=0, tiled=True)
    pair_input = returned_grad.reshape(-1, model_width)[targets].astype(jnp.float32)
    tokens_grad = jnp.sum(pair_input.reshape(tok_count, top_count, model_width), axis=1).astype(
        jnp.bfloat16
    )
    row_block = arrived.reshape(-1, model_width)
    column_block = row_block
    gate_sum = lax.psum_scatter(
        lax.dot_general(
            column_block, gate_pre_grad, contract_rows, preferred_element_type=jnp.float32
        ).astype(jnp.bfloat16),
        "dp",
        scatter_dimension=0,
        tiled=True,
    )
    column_block = row_block
    up_sum = lax.psum_scatter(
        lax.dot_general(
            column_block, up_pre_grad, contract_rows, preferred_element_type=jnp.float32
        ).astype(jnp.bfloat16),
        "dp",
        scatter_dimension=0,
        tiled=True,
    )
    column_block = incoming
    down_sum = (
        lax.psum_scatter(
            lax.dot_general(
                column_block, hidden, contract_rows, preferred_element_type=jnp.float32
            ).astype(jnp.bfloat16),
            "dp",
            scatter_dimension=0,
            tiled=True,
        )
        .astype(jnp.float32)
        .T
    )
    return (
        layer_out,
        tokens_grad,
        gate_sum[None],
        up_sum[None],
        down_sum.astype(jnp.bfloat16)[None],
    )


def solution(mesh):
    placed = (
        P(("dp", "expert"), None),
        P(("dp", "expert"), None),
        P(("dp", "expert"), None),
        P("expert", None, None),
        P("expert", None, None),
        P("expert", None, None),
        P(("dp", "expert"), None),
    )
    return jax.shard_map(
        per_device,
        mesh=mesh,
        in_specs=placed,
        out_specs=(
            P(("dp", "expert"), None),
            P(("dp", "expert"), None),
            P("expert", "dp", None),
            P("expert", "dp", None),
            P("expert", None, "dp"),
        ),
        check_vma=False,
    )
```

profile of v0, /device:TPU:0, one launch (start us, length us, event | category | flops | bytes accessed | tf_op | source)
XLA Modules:
  0.0 404.6 jit_solution(15272280271444568787)
XLA Ops:
  7.2 0.8 broadcast_multiply_fusion
  8.0 0.8 copy.16
  8.7 0.1 eq.29
  8.9 0.1 eq.25
  9.0 0.7 convert_multiply_fusion.1
  9.7 0.1 copy.14
  9.8 0.1 div.22
  10.0 0.1 copy.15
  10.1 0.1 mul.64
  10.2 0.6 reduce-window.6
  10.8 0.2 slice_reduce_fusion
  11.1 0.1 fusion.20
  11.2 1.4 scatter_custom_fusion
  12.6 2.8 gather_fusion.2
  15.5 0.1 mul.69
  15.5 4.1 %gather_fusion.3 = bf16[384,4096]{1,0:T(8,128)(2,1)} fusion(bf16[128,4096]{1,0:T(8,128)(2,1)S(1)} %copy-done, s32[1024]{0:T(1024)S(1)} %get-tuple-element.23), kind=kCustom, calls=%fused_computation.3 | custom fusion | bytes 6292992 | tf_op jit(solution)/shard_map/gather | solution.py:63
  19.6 4.6 %fusion = bf16[8,48,4096]{2,1,0:T(8,128)(2,1)} fusion(bf16[8,48,4096]{2,1,0:T(8,128)(2,1)} %bitcast.60, f32[8,48]{1,0:T(8,128)S(1)} %mul.69), kind=kLoop, calls=%fused_computation.10 | loop fusion | flops 4718592 | bytes 6292992 | tf_op jit(solution)/shard_map/convert_element_type | solution.py:64
  24.2 7.4 %all-to-all-start.2 = ((bf16[8,48,4096]{2,1,0:T(8,128)(2,1)}), bf16[8,48,4096]{2,1,0:T(8,128)(2,1)}, u32[]{:S(2)}, u32[]{:S(2)}) async-start(bf16[8,48,4096]{2,1,0:T(8,128)(2,1)} %fusion), calls=%async_computation.2 | async-start | bytes 6291456 | tf_op jit(solution)/shard_map/all_to_all | solution.py:66
  31.6 0.1 broadcast_in_dim.45
  31.7 4.0 gather_fusion
  35.7 3.9 broadcast_select_fusion
  39.6 62.8 %all-to-all-done.2 = bf16[8,48,4096]{2,1,0:T(8,128)(2,1)} async-done(((bf16[8,48,4096]{2,1,0:T(8,128)(2,1)}), bf16[8,48,4096]{2,1,0:T(8,128)(2,1)}, u32[]{:S(2)}, u32[]{:S(2)}) %all-to-all-start.2) | async-done | bytes 3145760 | tf_op jit(solution)/shard_map/all_to_all | solution.py:66
  102.4 3.6 all-to-all-start
  106.1 0.5 reduce-scatter.8.cloned.1.call-start
  106.6 7.4 %fusion.1 = f32[384,768]{1,0:T(8,128)} fusion(bf16[384,4096]{1,0:T(8,128)(2,1)} %bitcast.12, bf16[1,768,4096]{2,1,0:T(8,128)(2,1)} %param.12), kind=kOutput, calls=%fused_computation.11 | convolution fusion | flops 2415919104 | bytes 10616832 | tf_op jit(solution)/shard_map/dot_general | solution.py:74
  114.0 63.0 %all-to-all-done = bf16[8,48,4096]{2,1,0:T(8,128)(2,1)S(1)} async-done(((bf16[8,48,4096]{2,1,0:T(8,128)(2,1)}), bf16[8,48,4096]{2,1,0:T(8,128)(2,1)S(1)}, u32[]{:S(2)}, u32[]{:S(2)}) %all-to-all-start) | async-done | bytes 3145760 | tf_op jit(solution)/shard_map/all_to_all | solution.py:40
  176.9 5.5 %fusion.7 = f32[384,768]{1,0:T(8,128)S(1)} fusion(bf16[384,4096]{1,0:T(8,128)(2,1)S(1)} %bitcast.61, bf16[1,4096,768]{2,1,0:T(8,128)(2,1)} %param.11), kind=kOutput, calls=%fused_computation.17 | convolution fusion | flops 2415919104 | bytes 10616832 | tf_op jit(solution)/shard_map/dot_general | solution.py:44
  182.4 6.8 %multiply_convert_fusion.1 = (bf16[384,768]{1,0:T(8,128)(2,1)}, bf16[384,768]{1,0:T(8,128)(2,1)}, bf16[384,768]{1,0:T(8,128)(2,1)S(1)}) fusion(f32[384,768]{1,0:T(8,128)S(1)} %copy-done.6, f32[384,768]{1,0:T(8,128)S(1)} %fusion.7, bf16[384,4096]{1,0:T(8,128)(2,1)S(1)} %bitcast.62, bf16[1,4096,768]{2,1,0:T(8,128)(2,1)} %param.10), kind=kOutput, calls=%fused_computation.28 | convolution fusion | flops 2420342784 | bytes 13565952 | tf_op jit(solution)/shard_map/dot_general | solution.py:43
  189.2 0.8 copy-done.4
  190.0 8.0 %convolution_convert_fusion = bf16[4096,768]{1,0:T(8,128)(2,1)} fusion(bf16[384,4096]{1,0:T(8,128)(2,1)} %bitcast.12, bf16[384,768]{1,0:T(8,128)(2,1)S(1)} %get-tuple-element.19), kind=kOutput, calls=%fused_computation.6 | convolution fusion | flops 2419064832 | bytes 10027008 | tf_op jit(solution)/shard_map/dot_general | solution.py:115
  198.1 6.4 %convolution_convert_fusion.2 = bf16[4096,768]{1,0:T(8,128)(2,1)} fusion(bf16[384,4096]{1,0:T(8,128)(2,1)S(1)} %bitcast.63, bf16[384,768]{1,0:T(8,128)(2,1)} %get-tuple-element.17), kind=kOutput, calls=%fused_computation.8 | convolution fusion | flops 2419064832 | bytes 10027008 | tf_op jit(solution)/shard_map/dot_general | solution.py:96
  204.6 0.2 reduce-scatter.6.cloned.1.call-start
  204.8 6.7 %convolution_convert_fusion.1 = bf16[4096,768]{1,0:T(8,128)(2,1)} fusion(bf16[384,4096]{1,0:T(8,128)(2,1)S(1)} %bitcast.64, bf16[384,768]{1,0:T(8,128)(2,1)} %get-tuple-element.18), kind=kOutput, calls=%fused_computation.7 | convolution fusion | flops 2419064832 | bytes 10027008 | tf_op jit(solution)/shard_map/dot_general | solution.py:105
  211.5 1.0 copy-done.5
  212.5 6.8 %fusion.15 = bf16[384,4096]{1,0:T(8,128)(2,1)} fusion(bf16[384,768]{1,0:T(8,128)(2,1)S(1)} %copy-done.5, bf16[1,768,4096]{2,1,0:T(8,128)(2,1)} %param.12), kind=kOutput, calls=%fused_computation.24 | convolution fusion | flops 2417491968 | bytes 10027008 | tf_op jit(solution)/shard_map/dot_general | solution.py:46
  219.3 3.7 all-to-all-start.1
  223.0 4.9 %fusion.5 = f32[384,4096]{1,0:T(8,128)S(1)} fusion(bf16[384,768]{1,0:T(8,128)(2,1)} %get-tuple-element.18, bf16[1,4096,768]{2,1,0:T(8,128)(2,1)} %param.11), kind=kOutput, calls=%fused_computation.15 | convolution fusion | flops 2415919104 | bytes 13172736 | tf_op jit(solution)/shard_map/dot_general | solution.py:84
  227.9 8.5 %add_convert_fusion = bf16[384,4096]{1,0:T(8,128)(2,1)} fusion(f32[384,4096]{1,0:T(8,128)S(1)} %fusion.5, bf16[384,768]{1,0:T(8,128)(2,1)S(1)} %copy-done.3, bf16[1,4096,768]{2,1,0:T(8,128)(2,1)} %param.10), kind=kOutput, calls=%fused_computation.23 | convolution fusion | flops 2419064832 | bytes 16318464 | tf_op jit(solution)/shard_map/dot_general | solution.py:81
  236.5 57.5 %all-to-all-done.1 = bf16[8,48,4096]{2,1,0:T(8,128)(2,1)S(1)} async-done(((bf16[8,48,4096]{2,1,0:T(8,128)(2,1)}), bf16[8,48,4096]{2,1,0:T(8,128)(2,1)S(1)}, u32[]{:S(2)}, u32[]{:S(2)}) %all-to-all-start.1) | async-done | bytes 3145760 | tf_op jit(solution)/shard_map/all_to_all | solution.py:50
  294.0 4.4 %all-to-all-start.3 = ((bf16[8,48,4096]{2,1,0:T(8,128)(2,1)}), bf16[8,48,4096]{2,1,0:T(8,128)(2,1)}, u32[]{:S(2)}, u32[]{:S(2)}) async-start(bf16[8,48,4096]{2,1,0:T(8,128)(2,1)} %bitcast.65), calls=%async_computation.3 | async-start | bytes 6291456 | tf_op jit(solution)/shard_map/all_to_all | solution.py:88
  298.4 3.2 gather_fusion.1
  301.6 5.5 %reshape.118 = f32[128,2,4096]{2,1,0:T(2,128)} reshape(bf16[256,4096]{1,0:T(8,128)(2,1)} %gather_fusion.1) | data formatting | bytes 6291456 | tf_op jit(solution)/shard_map/convert_element_type | solution.py:58
  307.1 61.5 %all-to-all-done.3 = bf16[8,48,4096]{2,1,0:T(8,128)(2,1)} async-done(((bf16[8,48,4096]{2,1,0:T(8,128)(2,1)}), bf16[8,48,4096]{2,1,0:T(8,128)(2,1)}, u32[]{:S(2)}, u32[]{:S(2)}) %all-to-all-start.3) | async-done | bytes 3145760 | tf_op jit(solution)/shard_map/all_to_all | solution.py:88
  368.6 6.2 %gather_fusion.4 = bf16[256,4096]{1,0:T(8,128)(2,1)S(1)} fusion(bf16[384,4096]{1,0:T(8,128)(2,1)} %bitcast.14, s32[1024]{0:T(1024)S(1)} %pad_clamp_fusion.1), kind=kCustom, calls=%fused_computation.4 | custom fusion | bytes 4195328 | tf_op jit(solution)/shard_map/gather | solution.py:89
  374.8 2.9 gather.25
  377.7 7.9 %reduce_sum.35 = bf16[128,4096]{1,0:T(8,128)(2,1)} reduce(bf16[128,2,4096]{2,1,0:T(2,128)(2,1)} %gather.25, bf16[]{:T(256)} %constant.39.clone.1), dimensions={1}, to_apply=%region_5.6 | reduce | flops 524288 | bytes 3145730 | tf_op jit(solution)/shard_map/reduce_sum | solution.py:90
  385.6 9.6 %multiply_reduce_fusion = bf16[128,4096]{1,0:T(8,128)(2,1)} fusion(f32[128,2,4096]{2,1,0:T(2,128)} %reshape.118, f32[128,2]{1,0:T(8,128)S(1)} %copy.14), kind=kLoop, calls=%fused_computation.25 | loop fusion | flops 1572864 | bytes 5243904 | tf_op jit(solution)/shard_map/reduce_sum | solution.py:60
  395.2 2.6 copy.19
  (28 shorter events, 0.2 us)
Async XLA Ops:
  7.2 8.4 %copy-start = (bf16[128,4096]{1,0:T(8,128)(2,1)S(1)}, bf16[128,4096]{1,0:T(8,128)(2,1)}, u32[]{:S(2)}) copy-start(bf16[128,4096]{1,0:T(8,128)(2,1)} %param.13) | copy-start | bytes 3145732
  24.2 7.5 %copy-start.2 = (bf16[128,4096]{1,0:T(8,128)(2,1)S(1)}, bf16[128,4096]{1,0:T(8,128)(2,1)}, u32[]{:S(2)}) copy-start(bf16[128,4096]{1,0:T(8,128)(2,1)} %param.7) | copy-start | bytes 3145732
  24.2 78.2 %all-to-all-start.2 = ((bf16[8,48,4096]{2,1,0:T(8,128)(2,1)}), bf16[8,48,4096]{2,1,0:T(8,128)(2,1)}, u32[]{:S(2)}, u32[]{:S(2)}) async-start(bf16[8,48,4096]{2,1,0:T(8,128)(2,1)} %fusion), calls=%async_computation.2 | async-start | bytes 6291456 | tf_op jit(solution)/shard_map/all_to_all | solution.py:66
  102.4 74.5 %all-to-all-start = ((bf16[8,48,4096]{2,1,0:T(8,128)(2,1)}), bf16[8,48,4096]{2,1,0:T(8,128)(2,1)S(1)}, u32[]{:S(2)}, u32[]{:S(2)}) async-start(bf16[8,48,4096]{2,1,0:T(8,128)(2,1)} %broadcast_select_fusion), calls=%async_computation | async-start | bytes 6291456 | tf_op jit(solution)/shard_map/all_to_all | solution.py:40
  106.1 289.1 %reduce-scatter.8.cloned.1.call-start = ((), (), s32[]{:S(2)}) async-start(), calls=%async_computation.9 | async-start | bytes 7864320 | tf_op jit(solution)/shard_map/reduce_scatter | solution.py:114
  176.9 5.5 %copy-start.6 = (f32[384,768]{1,0:T(8,128)S(1)}, f32[384,768]{1,0:T(8,128)}, u32[]{:S(2)}) copy-start(f32[384,768]{1,0:T(8,128)} %fusion.1) | copy-start | bytes 3538948
  189.2 0.8 copy-start.4
  198.1 199.7 %reduce-scatter.4.cloned.1.call-start = ((), (), s32[]{:S(2)}) async-start(), calls=%async_computation.7 | async-start | bytes 7864320 | tf_op jit(solution)/shard_map/reduce_scatter | solution.py:95
  204.6 193.2 %reduce-scatter.6.cloned.1.call-start = ((), (), s32[]{:S(2)}) async-start(), calls=%async_computation.8 | async-start | bytes 7864320 | tf_op jit(solution)/shard_map/reduce_scatter | solution.py:104
  211.4 1.1 copy-start.5
  219.3 74.7 %all-to-all-start.1 = ((bf16[8,48,4096]{2,1,0:T(8,128)(2,1)}), bf16[8,48,4096]{2,1,0:T(8,128)(2,1)S(1)}, u32[]{:S(2)}, u32[]{:S(2)}) async-start(bf16[8,48,4096]{2,1,0:T(8,128)(2,1)} %bitcast.66), calls=%async_computation.1 | async-start | bytes 6291456 | tf_op jit(solution)/shard_map/all_to_all | solution.py:50
  223.0 5.0 %copy-start.3 = (bf16[384,768]{1,0:T(8,128)(2,1)S(1)}, bf16[384,768]{1,0:T(8,128)(2,1)}, u32[]{:S(2)}) copy-start(bf16[384,768]{1,0:T(8,128)(2,1)} %get-tuple-element.17) | copy-start | bytes 1769476
  294.0 74.6 %all-to-all-start.3 = ((bf16[8,48,4096]{2,1,0:T(8,128)(2,1)}), bf16[8,48,4096]{2,1,0:T(8,128)(2,1)}, u32[]{:S(2)}, u32[]{:S(2)}) async-start(bf16[8,48,4096]{2,1,0:T(8,128)(2,1)} %bitcast.65), calls=%async_computation.3 | async-start | bytes 6291456 | tf_op jit(solution)/shard_map/all_to_all | solution.py:88
  377.7 20.1 %copy-start.1 = (bf16[128,4096]{1,0:T(8,128)(2,1)S(1)}, bf16[128,4096]{1,0:T(8,128)(2,1)}, u32[]{:S(2)}) copy-start(bf16[128,4096]{1,0:T(8,128)(2,1)} %param.13) | copy-start | bytes 3145732
Sparse Core Ops, SparseCore 0:
  198.2 57.3 reduce-scatter.7
  258.9 58.3 reduce-scatter.3
  320.4 58.3 reduce-scatter.5
where the time goes:
time: 410 us; the launch traced here: 405 us
  waiting for transfers between devices  245 us (60%)
  matrix products  61 us (15%)
  local copies, waits for them, and re-layouts  36.4 us (9%)
  other arithmetic  28.2 us (7%)
  starting transfers between devices  20 us (5%)
  between operations  14.2 us (3%)
    all_to_all x1, waiting for transfers between devices, per_device(): lax.all_to_all(outbound, 'expert', split_axis=0, concat_axis=0, tiled=True)  63 us
    all_to_all x1, waiting for transfers between devices, per_device(): lax.all_to_all(pair_grad, 'expert', split_axis=0, concat_axis=0, tiled=True)  62.8 us
    all_to_all x1, waiting for transfers between devices, per_device(): lax.all_to_all(input_grad, 'expert', split_axis=0, concat_axis=0, tiled=T...  61.5 us
    all_to_all x1, waiting for transfers between devices, per_device(): lax.all_to_all(produced, 'expert', split_axis=0, concat_axis=0, tiled=True)  57.5 us
    reduce_sum x1, other arithmetic, per_device(): jnp.sum(weighted.reshape(tok_count, top_count, model_width), axis=1)  9.64 us
    gather x2, local copies, waits for them, and re-layouts, per_device(): returned_grad.reshape(-1, model_width)[targets].astype(jnp.float32)  9.04 us
    dot_general x1, matrix products, per_device(): lax.dot_general(gate_pre_grad, gate_matrix, contract, preferred_element_t...  8.54 us
  transfers between devices with their start and end apart: 7, of which 4 were waited for; matrix products, arithmetic and copies ran while one was open for 21% of the time, Pallas kernels for 0%

commit v1 on v0

--- a/solution.py
+++ b/solution.py
@@ -2,6 +2,17 @@
 import jax.numpy as jnp
 from jax import lax
 from jax.sharding import PartitionSpec as P
+
+
+def cut_along(shard, dim, size):
+    before, after = (shard.shape[:dim], shard.shape[dim + 1 :])
+    return jnp.moveaxis(shard.reshape(*before, size, -1, *after), dim, 0)
+
+
+def laid_out(tiles, dim):
+    tiles = jnp.moveaxis(tiles, 0, dim)
+    shape = tiles.shape
+    return tiles.reshape(*shape[:dim], shape[dim] * shape[dim + 1], *shape[dim + 2 :])
 
 
 def slot_targets(block_ids, experts, capacity):
@@ -85,7 +96,14 @@
         up_pre_grad, up_matrix, contract, preferred_element_type=jnp.float32
     )
     input_grad = input_grad.astype(jnp.bfloat16).reshape(experts, capacity, model_width)
-    returned_grad = lax.all_to_all(input_grad, "expert", split_axis=0, concat_axis=0, tiled=True)
+    size, place = (lax.axis_size("expert"), lax.axis_index("expert"))
+    blocks = cut_along(input_grad, 0, size)
+    outs = [blocks[place]]
+    for turn in range(1, size):
+        sent = blocks[place ^ turn]
+        outs.append(lax.ppermute(sent, "expert", [(i, i ^ turn) for i in range(size)]))
+    blocks = jnp.stack(outs)[place ^ jnp.arange(size)]
+    returned_grad = laid_out(blocks, 0)
     pair_input = returned_grad.reshape(-1, model_width)[targets].astype(jnp.float32)
     tokens_grad = jnp.sum(pair_input.reshape(tok_count, top_count, model_width), axis=1).astype(
         jnp.bfloat16

time: 410 us -> 450 us (1.098)
  starting transfers between devices: 20 us -> 41.4 us
  local copies, waits for them, and re-layouts: 36.4 us -> 52 us
  waiting for transfers between devices: 245 us -> 250 us
    ppermute x0 -> x7, waiting for transfers between devices: none -> 124 us  [per_device(): lax.ppermute(sent, 'expert', [(i, i ^ turn) for i in range(size)])]
    all_to_all x1 -> x0, waiting for transfers between devices: 61.5 us -> none  [per_device(): lax.all_to_all(input_grad, 'expert', split_axis=0, concat_axis=0, tiled=T...]
    all_to_all x1, waiting for transfers between devices: 57.5 us -> 0.01 us  [per_device(): lax.all_to_all(produced, 'expert', split_axis=0, concat_axis=0, tiled=True)]
    ppermute x0 -> x7, starting transfers between devices: none -> 13.8 us  [per_device(): lax.ppermute(sent, 'expert', [(i, i ^ turn) for i in range(size)])]
    reduce_scatter x1, starting transfers between devices: 0.21 us -> 12.3 us  [per_device(): lax.psum_scatter(lax.dot_general(column_block, up_pre_grad, contract_rows...]
    unnamed x16 -> x32, local copies, waits for them, and re-layouts: 5.24 us -> 10.9 us
  transfers between devices with their start and end apart: 7 -> 13, of which waited for: 4 -> 5; matrix products, arithmetic and copies ran while one was open for 21% -> 22% of each run, Pallas kernels for 0% -> 0%
where the time goes in v1:
time: 450 us; the launch traced here: 444 us
  waiting for transfers between devices  250 us (56%)
  matrix products  58.5 us (13%)
  local copies, waits for them, and re-layouts  52 us (12%)
  starting transfers between devices  41.4 us (9%)
  other arithmetic  27.9 us (6%)
  between operations  14.2 us (3%)
    ppermute x7, waiting for transfers between devices, per_device(): lax.ppermute(sent, 'expert', [(i, i ^ turn) for i in range(size)])  124 us
    all_to_all x1, waiting for transfers between devices, per_device(): lax.all_to_all(outbound, 'expert', split_axis=0, concat_axis=0, tiled=True)  63.1 us
    all_to_all x1, waiting for transfers between devices, per_device(): lax.all_to_all(pair_grad, 'expert', split_axis=0, concat_axis=0, tiled=True)  62.8 us
    ppermute x7, starting transfers between devices, per_device(): lax.ppermute(sent, 'expert', [(i, i ^ turn) for i in range(size)])  13.8 us
    reduce_scatter x1, starting transfers between devices, per_device(): lax.psum_scatter(lax.dot_general(column_block, up_pre_grad, contract_rows...  12.3 us
    gather x2, local copies, waits for them, and re-layouts, per_device(): returned_grad.reshape(-1, model_width)[targets].astype(jnp.float32)  12 us
    unnamed x32, local copies, waits for them, and re-layouts  10.9 us
    reduce_sum x1, other arithmetic, per_device(): jnp.sum(weighted.reshape(tok_count, top_count, model_width), axis=1)  9.64 us
  transfers between devices with their start and end apart: 13, of which 5 were waited for; matrix products, arithmetic and copies ran while one was open for 22% of the time, Pallas kernels for 0%

profile of v1, /device:TPU:0, one launch (start us, length us, event | category | flops | bytes accessed | tf_op | source)
XLA Modules:
  0.0 443.8 jit_solution(12038508680862612865)
XLA Ops:
  7.2 0.8 broadcast_multiply_fusion
  8.0 0.8 copy.16
  11.2 1.4 scatter_custom_fusion
  12.6 2.8 gather_fusion.2
  15.5 4.1 gather_fusion.3
  19.6 4.5 %fusion = bf16[8,48,4096]{2,1,0:T(8,128)(2,1)} fusion(bf16[8,48,4096]{2,1,0:T(8,128)(2,1)} %bitcast.92, f32[8,48]{1,0:T(8,128)S(1)} %mul.69), kind=kLoop, calls=%fused_computation.11 | loop fusion | flops 4718592 | bytes 6292992 | tf_op jit(solution)/shard_map/convert_element_type | solution.py:75
  24.1 7.4 %all-to-all-start.2 = ((bf16[8,48,4096]{2,1,0:T(8,128)(2,1)}), bf16[8,48,4096]{2,1,0:T(8,128)(2,1)}, u32[]{:S(2)}, u32[]{:S(2)}) async-start(bf16[8,48,4096]{2,1,0:T(8,128)(2,1)} %fusion), calls=%async_computation.2 | async-start | bytes 6291456 | tf_op jit(solution)/shard_map/all_to_all | solution.py:77
  31.6 4.1 gather_fusion
  35.7 3.8 broadcast_select_fusion
  39.5 62.8 %all-to-all-done.2 = bf16[8,48,4096]{2,1,0:T(8,128)(2,1)} async-done(((bf16[8,48,4096]{2,1,0:T(8,128)(2,1)}), bf16[8,48,4096]{2,1,0:T(8,128)(2,1)}, u32[]{:S(2)}, u32[]{:S(2)}) %all-to-all-start.2) | async-done | bytes 3145760 | tf_op jit(solution)/shard_map/all_to_all | solution.py:77
  102.4 3.6 all-to-all-start
  106.5 7.4 %fusion.1 = f32[384,768]{1,0:T(8,128)} fusion(bf16[384,4096]{1,0:T(8,128)(2,1)} %bitcast.12, bf16[1,768,4096]{2,1,0:T(8,128)(2,1)} %param.12), kind=kOutput, calls=%fused_computation.12 | convolution fusion | flops 2415919104 | bytes 10616832 | tf_op jit(solution)/shard_map/dot_general | solution.py:85
  113.8 63.1 %all-to-all-done = bf16[8,48,4096]{2,1,0:T(8,128)(2,1)S(1)} async-done(((bf16[8,48,4096]{2,1,0:T(8,128)(2,1)}), bf16[8,48,4096]{2,1,0:T(8,128)(2,1)S(1)}, u32[]{:S(2)}, u32[]{:S(2)}) %all-to-all-start) | async-done | bytes 3145760 | tf_op jit(solution)/shard_map/all_to_all | solution.py:51
  176.9 5.5 %fusion.7 = f32[384,768]{1,0:T(8,128)S(1)} fusion(bf16[384,4096]{1,0:T(8,128)(2,1)S(1)} %bitcast.95, bf16[1,4096,768]{2,1,0:T(8,128)(2,1)} %param.11), kind=kOutput, calls=%fused_computation.18 | convolution fusion | flops 2415919104 | bytes 10616832 | tf_op jit(solution)/shard_map/dot_general | solution.py:55
  182.4 6.8 %multiply_convert_fusion.1 = (bf16[384,768]{1,0:T(8,128)(2,1)}, bf16[384,768]{1,0:T(8,128)(2,1)}, bf16[384,768]{1,0:T(8,128)(2,1)S(1)}) fusion(f32[384,768]{1,0:T(8,128)S(1)} %copy-done.7, f32[384,768]{1,0:T(8,128)S(1)} %fusion.7, bf16[384,4096]{1,0:T(8,128)(2,1)S(1)} %bitcast.96, bf16[1,4096,768]{2,1,0:T(8,128)(2,1)} %param.10), kind=kOutput, calls=%fused_computation.29 | convolution fusion | flops 2420342784 | bytes 13565952 | tf_op jit(solution)/shard_map/dot_general | solution.py:54
  189.2 0.8 copy-done.4
  190.0 8.0 %convolution_convert_fusion = bf16[4096,768]{1,0:T(8,128)(2,1)} fusion(bf16[384,4096]{1,0:T(8,128)(2,1)} %bitcast.12, bf16[384,768]{1,0:T(8,128)(2,1)S(1)} %get-tuple-element.27), kind=kOutput, calls=%fused_computation.7 | convolution fusion | flops 2419064832 | bytes 10027008 | tf_op jit(solution)/shard_map/dot_general | solution.py:133
  198.1 6.4 %convolution_convert_fusion.2 = bf16[4096,768]{1,0:T(8,128)(2,1)} fusion(bf16[384,4096]{1,0:T(8,128)(2,1)S(1)} %bitcast.97, bf16[384,768]{1,0:T(8,128)(2,1)} %get-tuple-element.25), kind=kOutput, calls=%fused_computation.9 | convolution fusion | flops 2419064832 | bytes 10027008 | tf_op jit(solution)/shard_map/dot_general | solution.py:114
  204.5 12.3 %reduce-scatter.6.cloned.1.call-start = ((), (), s32[]{:S(2)}) async-start(), calls=%async_computation.7 | async-start | bytes 7864320 | tf_op jit(solution)/shard_map/reduce_scatter | solution.py:122
  216.8 6.4 %convolution_convert_fusion.1 = bf16[4096,768]{1,0:T(8,128)(2,1)} fusion(bf16[384,4096]{1,0:T(8,128)(2,1)S(1)} %bitcast.98, bf16[384,768]{1,0:T(8,128)(2,1)} %get-tuple-element.26), kind=kOutput, calls=%fused_computation.8 | convolution fusion | flops 2419064832 | bytes 10027008 | tf_op jit(solution)/shard_map/dot_general | solution.py:123
  223.3 1.0 copy-done.3
  224.3 9.0 %fusion.5 = f32[384,4096]{1,0:T(8,128)} fusion(bf16[384,768]{1,0:T(8,128)(2,1)S(1)} %copy-done.3, bf16[1,4096,768]{2,1,0:T(8,128)(2,1)} %param.11), kind=kOutput, calls=%fused_computation.16 | convolution fusion | flops 2415919104 | bytes 13172736 | tf_op jit(solution)/shard_map/dot_general | solution.py:95
  233.3 5.0 %add_convert_fusion = bf16[384,4096]{1,0:T(8,128)(2,1)S(1)} fusion(f32[384,4096]{1,0:T(8,128)} %fusion.5, bf16[384,768]{1,0:T(8,128)(2,1)S(1)} %copy-done.6, bf16[1,4096,768]{2,1,0:T(8,128)(2,1)S(1)} %bitcast.105), kind=kOutput, calls=%fused_computation.24 | convolution fusion | flops 2419064832 | bytes 16318464 | tf_op jit(solution)/shard_map/dot_general | solution.py:92
  238.3 1.7 dynamic-slice_bitcast_fusion
  240.0 1.5 collective-permute-start
  241.5 4.0 fusion.15
  245.5 3.8 all-to-all-start.1
  249.3 4.7 %collective-permute-start.6 = (bf16[1,48,4096]{2,1,0:T(8,128)(2,1)}, bf16[1,48,4096]{2,1,0:T(8,128)(2,1)S(1)}, u32[]{:S(2)}, u32[]{:S(2)}) collective-permute-start(bf16[1,48,4096]{2,1,0:T(8,128)(2,1)} %get-tuple-element.17), channel_id=1, source_target_pairs={{0,7},{1,6},{2,5},{3,4},{4,3},{5,2},{6,1},{7,0},{8,15},{9,14},{10,... | collective-permute-start | bytes 1179656 | tf_op jit(solution)/shard_map/ppermute | solution.py:104
  255.2 1.8 collective-permute-start.3
  257.0 1.4 collective-permute-start.1
  258.5 1.8 bitcast_dynamic-update-slice_fusion.6
  260.2 82.8 %collective-permute-done.1 = bf16[1,48,4096]{2,1,0:T(8,128)(2,1)S(1)} collective-permute-done((bf16[1,48,4096]{2,1,0:T(8,128)(2,1)}, bf16[1,48,4096]{2,1,0:T(8,128)(2,1)S(1)}, u32[]{:S(2)}, u32[]{:S(2)}) %collective-permute-start.1) | collective-permute-done | bytes 393248 | tf_op jit(solution)/shard_map/ppermute | solution.py:104
  343.0 3.2 collective-permute-start.2
  346.2 0.8 bitcast_dynamic-update-slice_fusion.5
  347.0 15.1 %collective-permute-done.2 = bf16[1,48,4096]{2,1,0:T(8,128)(2,1)S(1)} collective-permute-done((bf16[1,48,4096]{2,1,0:T(8,128)(2,1)}, bf16[1,48,4096]{2,1,0:T(8,128)(2,1)S(1)}, u32[]{:S(2)}, u32[]{:S(2)}) %collective-permute-start.2) | collective-permute-done | bytes 393248 | tf_op jit(solution)/shard_map/ppermute | solution.py:104
  362.9 26.0 %collective-permute-done.3 = bf16[1,48,4096]{2,1,0:T(8,128)(2,1)S(1)} collective-permute-done((bf16[1,48,4096]{2,1,0:T(8,128)(2,1)}, bf16[1,48,4096]{2,1,0:T(8,128)(2,1)S(1)}, u32[]{:S(2)}, u32[]{:S(2)}) %collective-permute-start.3) | collective-permute-done | bytes 393248 | tf_op jit(solution)/shard_map/ppermute | solution.py:104
  388.9 0.8 bitcast_dynamic-update-slice_fusion.3
  389.7 0.8 bitcast_dynamic-update-slice_fusion.2
  390.5 0.8 bitcast_dynamic-update-slice_fusion.1
  391.2 0.8 bitcast_dynamic-update-slice_fusion
  392.0 4.4 gather_fusion.4
  396.4 7.5 %gather_fusion.5 = bf16[256,4096]{1,0:T(8,128)(2,1)} fusion(bf16[384,4096]{1,0:T(8,128)(2,1)} %bitcast.90, s32[1024]{0:T(1024)S(1)} %pad_clamp_fusion.2), kind=kCustom, calls=%fused_computation.5 | custom fusion | bytes 4195328 | tf_op jit(solution)/shard_map/gather | solution.py:107
  403.9 4.4 gather.29
  408.4 7.7 %reduce_sum.35 = bf16[128,4096]{1,0:T(8,128)(2,1)} reduce(bf16[128,2,4096]{2,1,0:T(2,128)(2,1)} %gather.29, bf16[]{:T(256)} %constant.17.clone.1), dimensions={1}, to_apply=%region_5.6 | reduce | flops 524288 | bytes 3145730 | tf_op jit(solution)/shard_map/reduce_sum | solution.py:108
  416.1 3.2 gather_fusion.1
  419.3 5.6 %reshape.126 = f32[128,2,4096]{2,1,0:T(2,128)} reshape(bf16[256,4096]{1,0:T(8,128)(2,1)} %gather_fusion.1) | data formatting | bytes 6291456 | tf_op jit(solution)/shard_map/convert_element_type | solution.py:69
  424.8 9.6 %multiply_reduce_fusion = bf16[128,4096]{1,0:T(8,128)(2,1)} fusion(f32[128,2,4096]{2,1,0:T(2,128)} %reshape.126, f32[128,2]{1,0:T(8,128)S(1)} %copy.14), kind=kLoop, calls=%fused_computation.26 | loop fusion | flops 1572864 | bytes 5243904 | tf_op jit(solution)/shard_map/reduce_sum | solution.py:71
  434.5 2.6 copy.19
  (63 shorter events, 5.1 us)
Async XLA Ops:
  7.2 8.4 %copy-start = (bf16[128,4096]{1,0:T(8,128)(2,1)S(1)}, bf16[128,4096]{1,0:T(8,128)(2,1)}, u32[]{:S(2)}) copy-start(bf16[128,4096]{1,0:T(8,128)(2,1)} %param.13) | copy-start | bytes 3145732
  24.1 7.5 %copy-start.2 = (bf16[128,4096]{1,0:T(8,128)(2,1)S(1)}, bf16[128,4096]{1,0:T(8,128)(2,1)}, u32[]{:S(2)}) copy-start(bf16[128,4096]{1,0:T(8,128)(2,1)} %param.7) | copy-start | bytes 3145732
  24.1 78.2 %all-to-all-start.2 = ((bf16[8,48,4096]{2,1,0:T(8,128)(2,1)}), bf16[8,48,4096]{2,1,0:T(8,128)(2,1)}, u32[]{:S(2)}, u32[]{:S(2)}) async-start(bf16[8,48,4096]{2,1,0:T(8,128)(2,1)} %fusion), calls=%async_computation.2 | async-start | bytes 6291456 | tf_op jit(solution)/shard_map/all_to_all | solution.py:77
  102.4 74.5 %all-to-all-start = ((bf16[8,48,4096]{2,1,0:T(8,128)(2,1)}), bf16[8,48,4096]{2,1,0:T(8,128)(2,1)S(1)}, u32[]{:S(2)}, u32[]{:S(2)}) async-start(bf16[8,48,4096]{2,1,0:T(8,128)(2,1)} %broadcast_select_fusion), calls=%async_computation | async-start | bytes 6291456 | tf_op jit(solution)/shard_map/all_to_all | solution.py:51
  106.0 328.4 %reduce-scatter.8.cloned.1.call-start = ((), (), s32[]{:S(2)}) async-start(), calls=%async_computation.8 | async-start | bytes 7864320 | tf_op jit(solution)/shard_map/reduce_scatter | solution.py:132
  176.9 5.5 %copy-start.7 = (f32[384,768]{1,0:T(8,128)S(1)}, f32[384,768]{1,0:T(8,128)}, u32[]{:S(2)}) copy-start(f32[384,768]{1,0:T(8,128)} %fusion.1) | copy-start | bytes 3538948
  189.1 0.8 copy-start.4
  198.0 239.0 %reduce-scatter.4.cloned.1.call-start = ((), (), s32[]{:S(2)}) async-start(), calls=%async_computation.6 | async-start | bytes 7864320 | tf_op jit(solution)/shard_map/reduce_scatter | solution.py:113
  204.5 232.5 %reduce-scatter.6.cloned.1.call-start = ((), (), s32[]{:S(2)}) async-start(), calls=%async_computation.7 | async-start | bytes 7864320 | tf_op jit(solution)/shard_map/reduce_scatter | solution.py:122
  223.2 1.1 copy-start.3
  223.2 10.0 %slice-start = ((s8[6291456]{0:T(1024)(128)(4,1)}), s8[2097152]{0:T(1024)(128)(4,1)S(1)}, s32[]{:S(2)}) async-start(s8[6291456]{0:T(1024)(128)(4,1)} %bitcast.104), calls=%async_computation.9 | async-start | bytes 4194304
  224.3 9.0 %slice-start.1 = ((s8[6291456]{0:T(1024)(128)(4,1)}), s8[4194304]{0:T(1024)(128)(4,1)S(1)}, s32[]{:S(2)}) async-start(s8[6291456]{0:T(1024)(128)(4,1)} %bitcast.104), calls=%async_computation.10 | async-start | bytes 8388608
  224.3 9.0 %copy-start.6 = (bf16[384,768]{1,0:T(8,128)(2,1)S(1)}, bf16[384,768]{1,0:T(8,128)(2,1)}, u32[]{:S(2)}) copy-start(bf16[384,768]{1,0:T(8,128)(2,1)} %get-tuple-element.25) | copy-start | bytes 1769476
  224.3 17.2 %slice-start.2 = ((s8[6291456]{0:T(1024)(128)(4,1)}), s8[4194304]{0:T(1024)(128)(4,1)S(1)}, s32[]{:S(2)}) async-start(s8[6291456]{0:T(1024)(128)(4,1)} %bitcast.106), calls=%async_computation.11 | async-start | bytes 8388608
  233.3 8.2 %slice-start.3 = ((s8[6291456]{0:T(1024)(128)(4,1)}), s8[2097152]{0:T(1024)(128)(4,1)S(1)}, s32[]{:S(2)}) async-start(s8[6291456]{0:T(1024)(128)(4,1)} %bitcast.106), calls=%async_computation.12 | async-start | bytes 4194304
  238.3 3.2 copy-start.5
  240.0 17.0 %collective-permute-start = (bf16[1,48,4096]{2,1,0:T(8,128)(2,1)}, bf16[1,48,4096]{2,1,0:T(8,128)(2,1)}, u32[]{:S(2)}, u32[]{:S(2)}) collective-permute-start(bf16[1,48,4096]{2,1,0:T(8,128)(2,1)} %get-tuple-element.23), channel_id=1, source_target_pairs={{0,1},{1,0},{2,3},{3,2},{4,5},{5,4},{6,7},{7,6},{8,9},{9,8},{10,11... | collective-permute-start | bytes 1179656 | tf_op jit(solution)/shard_map/ppermute | solution.py:104
  245.5 170.5 %all-to-all-start.1 = ((bf16[8,48,4096]{2,1,0:T(8,128)(2,1)}), bf16[8,48,4096]{2,1,0:T(8,128)(2,1)S(1)}, u32[]{:S(2)}, u32[]{:S(2)}) async-start(bf16[8,48,4096]{2,1,0:T(8,128)(2,1)} %bitcast.94), calls=%async_computation.1 | async-start | bytes 6291456 | tf_op jit(solution)/shard_map/all_to_all | solution.py:61
  249.3 141.9 %collective-permute-start.6 = (bf16[1,48,4096]{2,1,0:T(8,128)(2,1)}, bf16[1,48,4096]{2,1,0:T(8,128)(2,1)S(1)}, u32[]{:S(2)}, u32[]{:S(2)}) collective-permute-start(bf16[1,48,4096]{2,1,0:T(8,128)(2,1)} %get-tuple-element.17), channel_id=1, source_target_pairs={{0,7},{1,6},{2,5},{3,4},{4,3},{5,2},{6,1},{7,0},{8,15},{9,14},{10,... | collective-permute-start | bytes 1179656 | tf_op jit(solution)/shard_map/ppermute | solution.py:104
  254.1 136.4 %collective-permute-start.5 = (bf16[1,48,4096]{2,1,0:T(8,128)(2,1)}, bf16[1,48,4096]{2,1,0:T(8,128)(2,1)S(1)}, u32[]{:S(2)}, u32[]{:S(2)}) collective-permute-start(bf16[1,48,4096]{2,1,0:T(8,128)(2,1)} %get-tuple-element.18), channel_id=1, source_target_pairs={{0,6},{1,7},{2,4},{3,5},{4,2},{5,3},{6,0},{7,1},{8,14},{9,15},{10,... | collective-permute-start | bytes 1179656 | tf_op jit(solution)/shard_map/ppermute | solution.py:104
  254.6 135.0 %collective-permute-start.4 = (bf16[1,48,4096]{2,1,0:T(8,128)(2,1)}, bf16[1,48,4096]{2,1,0:T(8,128)(2,1)S(1)}, u32[]{:S(2)}, u32[]{:S(2)}) collective-permute-start(bf16[1,48,4096]{2,1,0:T(8,128)(2,1)} %get-tuple-element.19), channel_id=1, source_target_pairs={{0,5},{1,4},{2,7},{3,6},{4,1},{5,0},{6,3},{7,2},{8,13},{9,12},{10,... | collective-permute-start | bytes 1179656 | tf_op jit(solution)/shard_map/ppermute | solution.py:104
  255.2 133.7 %collective-permute-start.3 = (bf16[1,48,4096]{2,1,0:T(8,128)(2,1)}, bf16[1,48,4096]{2,1,0:T(8,128)(2,1)S(1)}, u32[]{:S(2)}, u32[]{:S(2)}) collective-permute-start(bf16[1,48,4096]{2,1,0:T(8,128)(2,1)} %get-tuple-element.20), channel_id=1, source_target_pairs={{0,4},{1,5},{2,6},{3,7},{4,0},{5,1},{6,2},{7,3},{8,12},{9,13},{10,... | collective-permute-start | bytes 1179656 | tf_op jit(solution)/shard_map/ppermute | solution.py:104
  257.0 86.0 %collective-permute-start.1 = (bf16[1,48,4096]{2,1,0:T(8,128)(2,1)}, bf16[1,48,4096]{2,1,0:T(8,128)(2,1)S(1)}, u32[]{:S(2)}, u32[]{:S(2)}) collective-permute-start(bf16[1,48,4096]{2,1,0:T(8,128)(2,1)} %get-tuple-element.22), channel_id=1, source_target_pairs={{0,2},{1,3},{2,0},{3,1},{4,6},{5,7},{6,4},{7,5},{8,10},{9,11},{10,... | collective-permute-start | bytes 1179656 | tf_op jit(solution)/shard_map/ppermute | solution.py:104
  343.0 19.1 %collective-permute-start.2 = (bf16[1,48,4096]{2,1,0:T(8,128)(2,1)}, bf16[1,48,4096]{2,1,0:T(8,128)(2,1)S(1)}, u32[]{:S(2)}, u32[]{:S(2)}) collective-permute-start(bf16[1,48,4096]{2,1,0:T(8,128)(2,1)} %get-tuple-element.21), channel_id=1, source_target_pairs={{0,3},{1,2},{2,1},{3,0},{4,7},{5,6},{6,5},{7,4},{8,11},{9,10},{10,... | collective-permute-start | bytes 1179656 | tf_op jit(solution)/shard_map/ppermute | solution.py:104
  419.3 17.8 %copy-start.1 = (bf16[128,4096]{1,0:T(8,128)(2,1)S(1)}, bf16[128,4096]{1,0:T(8,128)(2,1)}, u32[]{:S(2)}) copy-start(bf16[128,4096]{1,0:T(8,128)(2,1)} %param.13) | copy-start | bytes 3145732
Sparse Core Ops, SparseCore 0:
  198.1 57.4 reduce-scatter.7
  258.9 58.3 reduce-scatter.3
  320.4 58.3 reduce-scatter.5
